TPU v7x, 256 devices: a whole 4x4x8 slice. The times are simulated.
256 devices in a mesh: dp: 32 (over x, z), mp: 8 (over y, core).
Axes of the slice: x: 4, y: 4, z: 8, core: 2. Of those that a mesh axis runs over, the one named last changes fastest.
Arguments:
- grad_parts: bfloat16 [32, 16, 1024, 1024], P('dp', None, None, 'mp'), may hold values from -6 to 6
- owners: int32 [16], replicated, may hold values from 0 to 7, as said below
- left_stat: float32 [32, 1024, 1024], P('mp', 'dp'), may hold values from -1 to 8
- right_stat: float32 [32, 1024, 1024], P('mp', 'dp'), may hold values from -1 to 8
- left_root: bfloat16 [32, 1024, 1024], P('mp', 'dp'), may hold values from -1 to 9
- right_root: bfloat16 [32, 1024, 1024], P('mp'), may hold values from -1 to 3
- first_moment: float32 [32, 1024, 1024], P('mp', 'dp'), may hold values from -32 to 32
- second_moment: float32 [32, 1024, 1024], P('mp', 'dp'), may hold values from 0.5 to 2
- vec_grad: bfloat16 [32, 73728], P('dp', 'mp'), may hold values from -3 to 3
- vec_first: float32 [73728], P('mp'), may hold values from -4 to 4
- vec_second: float32 [73728], P('mp'), may hold values from 0.5 to 2
Outputs:
- block_update: bfloat16 [16, 1024, 1024], P(None, 'dp', 'mp')
- left_new: float32 [32, 1024, 1024], P('mp', 'dp')
- right_new: float32 [32, 1024, 1024], P('mp', 'dp')
- first_new: float32 [32, 1024, 1024], P('mp', 'dp')
- second_new: float32 [32, 1024, 1024], P('mp', 'dp')
- vec_update: bfloat16 [73728], P('mp')
- vec_first_new: float32 [73728], P('mp')
- vec_second_new: float32 [73728], P('mp')
Inputs may be any that keep to these rules, and one draw needn't show every extreme that they name: `owners`: no owner holds more than 4 blocks, and in every draw some owner holds exactly 4.
All inputs are finite; a program needn't handle non-finite values.
Results may differ from a plain program's by a relative error of at most 0.018.
Values may be sent and summed in bfloat16 or wider, within the bound.
A program may use at most 128 MiB of HBM per device.

v0:
```python
import jax
import jax.numpy as jnp
from jax import lax
from jax.sharding import PartitionSpec as P

beta_one = 0.9
beta_two = 0.95
adam_eps = 1e-08
graft_eps = 1e-06


def owner_table(owners, owner_count, slot_count):
    block_count = owners.shape[0]
    same = owners[:, None] == owners[None, :]
    earlier = lax.broadcasted_iota(jnp.int32, (block_count, block_count), 1) < lax.broadcasted_iota(
        jnp.int32, (block_count, block_count), 0
    )
    slots = jnp.sum((same & earlier).astype(jnp.int32), axis=1)
    owner_ids = lax.broadcasted_iota(jnp.int32, (owner_count, slot_count, block_count), 0)
    slot_ids = lax.broadcasted_iota(jnp.int32, (owner_count, slot_count, block_count), 1)
    return ((owners[None, None, :] == owner_ids) & (slots[None, None, :] == slot_ids)).astype(
        jnp.float32
    )


def body(
    grad_parts,
    owners,
    left_stat,
    right_stat,
    left_root,
    right_root,
    first_moment,
    second_moment,
    vec_grad,
    vec_first,
    vec_second,
):
    owner_count = lax.axis_size("mp")
    slot_count, row_count, order = left_stat.shape
    col_count = order // owner_count
    my_rows = lax.axis_index("dp") * row_count
    my_owner = lax.axis_index("mp")
    row_pieces = lax.psum_scatter(
        grad_parts[0].astype(jnp.float32).astype(jnp.bfloat16),
        "dp",
        scatter_dimension=1,
        tiled=True,
    ).astype(jnp.float32)
    selector = owner_table(owners, owner_count, slot_count)
    outgoing = jnp.einsum("ocb,brw->crow", selector, row_pieces, precision=lax.Precision.HIGHEST)
    incoming = lax.all_to_all(
        outgoing.astype(jnp.bfloat16), "mp", split_axis=2, concat_axis=2, tiled=True
    ).astype(outgoing.dtype)
    grad_rows = incoming.reshape(slot_count, row_count, order)
    mine = lax.dynamic_index_in_dim(selector, my_owner, 0, keepdims=False)
    used_mask = (jnp.sum(mine, axis=1) > 0.5)[:, None, None]
    rounded_rows = grad_rows.astype(jnp.bfloat16)
    shard_rows = lax.all_gather(rounded_rows, "dp", axis=1, tiled=True)
    left_part = jnp.einsum(
        "crk,cnk->crn", rounded_rows, shard_rows, preferred_element_type=jnp.float32
    )
    own_cols = lax.dynamic_slice_in_dim(shard_rows, my_rows, row_count, 2)
    right_acc = jnp.einsum("cnr,cnk->crk", own_cols, shard_rows, preferred_element_type=jnp.float32)
    applied_acc = jnp.einsum(
        "crn,cnk->crk", left_root, shard_rows, preferred_element_type=jnp.float32
    )
    scale = 1.0 / order
    left_new = jnp.where(used_mask, left_stat + left_part * scale, left_stat)
    right_new = jnp.where(used_mask, right_stat + right_acc * scale, right_stat)
    first_new = jnp.where(
        used_mask, beta_one * first_moment + (1.0 - beta_one) * grad_rows, first_moment
    )
    second_new = jnp.where(
        used_mask,
        beta_two * second_moment + (1.0 - beta_two) * grad_rows * grad_rows,
        second_moment,
    )
    adam = first_new / (jnp.sqrt(second_new) + adam_eps)
    precond = jnp.einsum(
        "crk,ckm->crm",
        applied_acc.astype(jnp.bfloat16),
        right_root,
        preferred_element_type=jnp.float32,
    )
    square_adam = jnp.sum(adam * adam, axis=(1, 2))
    square_pre = jnp.sum(precond * precond, axis=(1, 2))
    vec_local = vec_grad[0].astype(jnp.float32)
    square_adam, square_pre, vec_sum = lax.psum((square_adam, square_pre, vec_local), "dp")
    cells = float(order * order)
    graft = jnp.sqrt(square_adam / cells) / jnp.sqrt(square_pre / cells + graft_eps)
    update_rows = (precond * graft[:, None, None]).astype(jnp.bfloat16)
    returned = lax.all_to_all(
        update_rows.reshape(slot_count, row_count, owner_count, col_count),
        "mp",
        split_axis=2,
        concat_axis=2,
        tiled=True,
    )
    block_update = jnp.einsum(
        "ocb,crow->brw", selector.astype(jnp.bfloat16), returned, preferred_element_type=jnp.float32
    ).astype(jnp.bfloat16)
    vec_first_new = beta_one * vec_first + (1.0 - beta_one) * vec_sum
    vec_second_new = beta_two * vec_second + (1.0 - beta_two) * vec_sum * vec_sum
    vec_update = (vec_first_new / (jnp.sqrt(vec_second_new) + adam_eps)).astype(jnp.bfloat16)
    return (
        block_update,
        left_new,
        right_new,
        first_new,
        second_new,
        vec_update,
        vec_first_new,
        vec_second_new,
    )


def solution(mesh):
    placed = (
        P("dp", None, None, "mp"),
        P(),
        P("mp", "dp", None),
        P("mp", "dp", None),
        P("mp", "dp", None),
        P("mp", None, None),
        P("mp", "dp", None),
        P("mp", "dp", None),
        P("dp", "mp"),
        P("mp"),
        P("mp"),
    )
    return jax.shard_map(
        body,
        mesh=mesh,
        in_specs=placed,
        out_specs=(
            P(None, "dp", "mp"),
            P("mp", "dp", None),
            P("mp", "dp", None),
            P("mp", "dp", None),
            P("mp", "dp", None),
            P("mp"),
            P("mp"),
            P("mp"),
        ),
        check_vma=False,
    )
```

profile of v0, /device:TPU:1, one launch (start us, length us, event | category | flops | bytes accessed | tf_op | source)
XLA Modules:
  0.0 519.0 jit_solution(16055392310687253301)
XLA Ops:
  7.2 0.0 reduce-scatter.2.cloned.1.call-start
  7.2 0.7 reduce-scatter.2.cloned.1.call-update
  7.9 0.0 all-gather.2.cloned.1.call-start
  8.0 0.9 convert_reduce_fusion
  8.9 224.1 %reduce-scatter.2.cloned.1.call-done = bf16[16,32,128]{2,1,0:T(8,128)(2,1)} async-done(((bf16[16,1024,128]{2,1,0:T(8,128)(2,1)}), bf16[16,32,128]{2,1,0:T(8,128)(2,1)}) %reduce-scatter.2.cloned.1.call-update) | async-done | bytes 131088 | tf_op jit(solution)/shard_map/reduce_scatter | solution.py:44
  233.0 1.1 fusion.4
  234.2 16.5 %all_to_all.10 = bf16[4,32,8,128]{3,1,0,2:T(8,128)(2,1)S(1)} all-to-all(bf16[4,32,8,128]{3,1,0,2:T(8,128)(2,1)S(1)} %copy.31), channel_id=1, replica_groups=mesh['dp'=32,'mp'=8] {'mp'}, dimensions={2} | all-to-all | bytes 524288 | tf_op jit(solution)/shard_map/all_to_all | solution.py:52
  250.7 0.7 copy_bitcast_fusion
  251.4 0.0 all-gather.2.cloned.1.call-update
  251.4 0.8 convert_element_type.50
  252.2 0.7 fusion.19
  252.9 0.1 dynamic-slice_reduce_fusion
  253.0 2.6 multiply_reduce_fusion.1
  255.6 90.5 %all-gather.2.cloned.1.call-done = bf16[4,1024,1024]{2,1,0:T(8,128)(2,1)} async-done(((bf16[4,32,1024]{2,1,0:T(8,128)(2,1)}), bf16[4,1024,1024]{2,1,0:T(8,128)(2,1)}) %all-gather.2.cloned.1.call-update) | async-done | bytes 8388624 | tf_op jit(solution)/shard_map/all_gather | solution.py:59
  346.1 8.9 %multiply_reduce_fusion = (f32[4]{0:T(128)S(1)}, f32[4,32,1024]{2,1,0:T(8,128)S(1)}) fusion(bf16[4,1024,1024]{2,1,0:T(8,128)(2,1)} %param.16, bf16[4,32,1024]{2,1,0:T(8,128)(2,1)S(1)} %copy-done, bf16[4,1024,1024]{2,1,0:T(8,128)(2,1)} %all-gather.2.cloned.1.call-done), kind=kOutput, calls=%fused_computation.20 | convolution fusion | flops 537264128 | bytes 17563664 | tf_op jit(solution)/shard_map/crk,ckm->crm/dot_general | solution.py:80
  355.0 112.0 %all-reduce = (f32[4]{0:T(128)S(1)}, f32[4]{0:T(128)S(1)}, f32[9216]{0:T(1024)S(1)}) all-reduce(f32[4]{0:T(128)S(1)} %get-tuple-element.41, f32[4]{0:T(128)S(1)} %get-tuple-element.38, f32[9216]{0:T(1024)S(1)} %bitcast.49), channel_id=1, replica_groups=mesh['dp'=32,'mp'=8] {'dp'}, use_global_device_ids=true, to_apply=%region_6.7 | all-reduce | flops 9224 | bytes 73792 | tf_op jit(solution)/shard_map/psum | solution.py:89
  467.0 0.1 multiply_convert_fusion
  467.2 0.9 copy.33
  468.1 32.8 %all-to-all-start.1 = ((bf16[4,32,8,128]{3,0,1,2:T(4,128)(2,1)}), bf16[4,32,8,128]{3,0,1,2:T(4,128)(2,1)S(1)}, u32[]{:S(2)}, u32[]{:S(2)}) async-start(bf16[4,32,8,128]{3,0,1,2:T(4,128)(2,1)} %copy.33), calls=%async_computation.2 | async-start | bytes 524288 | tf_op jit(solution)/shard_map/all_to_all | solution.py:93
  501.0 6.9 %fusion.1 = f32[4,32,1024]{2,1,0:T(8,128)} fusion(f32[4,32,1024]{2,1,0:T(8,128)S(1)} %copy-done.2, bf16[4,1024,1024]{2,1,0:T(8,128)(2,1)} %all-gather.2.cloned.1.call-done, pred[4]{0:T(512)(128)(4,1)S(1)} %broadcast_compare_fusion, bf16[4,32,8,128]{3,1,0,2:T(8,128)(2,1)S(1)} %all_to_all.10), kind=kOutput, calls=%fused_computation.3 | convolution fusion | flops 268828672 | bytes 9699332 | tf_op jit(solution)/shard_map/crk,cnk->crn/dot_general | solution.py:60
  507.9 2.6 fusion.3
  510.5 0.6 divide_convert_fusion
  511.2 0.3 fusion.5
  511.4 0.7 copy.36
  (19 shorter events, 0.1 us)
Async XLA Ops:
  7.2 338.9 %copy-start = (bf16[4,32,1024]{2,1,0:T(8,128)(2,1)S(1)}, bf16[4,32,1024]{2,1,0:T(8,128)(2,1)}, u32[]{:S(2)}) copy-start(bf16[4,32,1024]{2,1,0:T(8,128)(2,1)} %param.15) | copy-start | bytes 786436
  7.2 225.8 %reduce-scatter.2.cloned.1.call-start = ((), (), s32[]{:S(2)}) async-start(), calls=%async_computation.3 | async-start | bytes 4325376 | tf_op jit(solution)/shard_map/reduce_scatter | solution.py:44
  7.9 338.2 %all-gather.2.cloned.1.call-start = ((), (), s32[]{:S(2)}) async-start(), calls=%async_computation.4 | async-start | bytes 8650752 | tf_op jit(solution)/shard_map/all_gather | solution.py:59
  255.6 245.3 %copy-start.2 = (f32[4,32,1024]{2,1,0:T(8,128)S(1)}, f32[4,32,1024]{2,1,0:T(8,128)}, u32[]{:S(2)}) copy-start(f32[4,32,1024]{2,1,0:T(8,128)} %param.13) | copy-start | bytes 1572868
  355.0 152.9 %copy-start.3 = (f32[4,32,1024]{2,1,0:T(8,128)S(1)}, f32[4,32,1024]{2,1,0:T(8,128)}, u32[]{:S(2)}) copy-start(f32[4,32,1024]{2,1,0:T(8,128)} %param.14) | copy-start | bytes 1572868
  468.1 43.1 %all-to-all-start.1 = ((bf16[4,32,8,128]{3,0,1,2:T(4,128)(2,1)}), bf16[4,32,8,128]{3,0,1,2:T(4,128)(2,1)S(1)}, u32[]{:S(2)}, u32[]{:S(2)}) async-start(bf16[4,32,8,128]{3,0,1,2:T(4,128)(2,1)} %copy.33), calls=%async_computation.2 | async-start | bytes 524288 | tf_op jit(solution)/shard_map/all_to_all | solution.py:93
  500.9 7.0 %copy-start.1 = (bf16[4,1024,1024]{2,1,0:T(8,128)(2,1)S(1)}, bf16[4,1024,1024]{2,1,0:T(8,128)(2,1)}, u32[]{:S(2)}) copy-start(bf16[4,1024,1024]{2,1,0:T(8,128)(2,1)} %all-gather.2.cloned.1.call-done) | copy-start | bytes 25165828
  500.9 9.6 %copy-start.4 = (f32[9216]{0:T(1024)S(1)}, f32[9216]{0:T(1024)}, u32[]{:S(2)}) copy-start(f32[9216]{0:T(1024)} %param.21) | copy-start | bytes 110596
  500.9 9.6 %copy-start.5 = (f32[9216]{0:T(1024)S(1)}, f32[9216]{0:T(1024)}, u32[]{:S(2)}) copy-start(f32[9216]{0:T(1024)} %param.20) | copy-start | bytes 110596
  500.9 10.2 %copy-start.6 = (s32[16]{0:T(128)S(1)}, s32[16]{0:T(128)}, u32[]{:S(2)}) copy-start(s32[16]{0:T(128)} %param.12) | copy-start | bytes 196
Sparse Core Ops, SparseCore 0:
  11.9 221.0 reduce-scatter.1
  251.5 94.4 all-gather.1
where the time goes:
time: 519 us
  waiting for transfers between devices  315 us (61%)
  blocking collectives  129 us (25%)
  starting transfers between devices  32.9 us (6%)
  matrix products  19.8 us (4%)
  between operations  14.1 us (3%)
  other arithmetic  5.83 us (1%)
    reduce_scatter x1, waiting for transfers between devices, body(): lax.psum_scatter(grad_parts[0].astype(jnp.float32).astype(jnp.bfloat16),...  224 us
    psum x1, blocking collectives, body(): lax.psum((square_adam, square_pre, vec_local), 'dp')  112 us
    all_gather x1, waiting for transfers between devices, body(): shard_rows = lax.all_gather(rounded_rows, 'dp', axis=1, tiled=True)  90.5 us
    all_to_all x1, starting transfers between devices, body(): lax.all_to_all(update_rows.reshape(slot_count, row_count, owner_count, co...  32.8 us
    all_to_all x1, blocking collectives, body(): lax.all_to_all(outgoing.astype(jnp.bfloat16), 'mp', split_axis=2, concat_...  16.5 us
  transfers between devices with their start and end apart: 3, of which 2 were waited for; matrix products, arithmetic and copies ran while one was open for 3% of the time, Pallas kernels for 0%

commit v1 on v0

--- a/solution.py
+++ b/solution.py
@@ -56,7 +56,9 @@
     mine = lax.dynamic_index_in_dim(selector, my_owner, 0, keepdims=False)
     used_mask = (jnp.sum(mine, axis=1) > 0.5)[:, None, None]
     rounded_rows = grad_rows.astype(jnp.bfloat16)
-    shard_rows = lax.all_gather(rounded_rows, "dp", axis=1, tiled=True)
+    shard_rows = jnp.concatenate(
+        lax.all_to_all(jnp.stack([rounded_rows] * lax.axis_size("dp")), "dp", 0, 0), axis=1
+    )
     left_part = jnp.einsum(
         "crk,cnk->crn", rounded_rows, shard_rows, preferred_element_type=jnp.float32
     )

time: 519 us -> 638 us (1.23)
  waiting for transfers between devices: 315 us -> 408 us
  starting transfers between devices: 32.9 us -> 46 us
  local copies, waits for them, and re-layouts: 2.49 us -> 14.5 us
    all_to_all x0 -> x1, waiting for transfers between devices: none -> 183 us  [body(): lax.all_to_all(jnp.stack([rounded_rows] * lax.axis_size('dp')), 'dp', 0, 0)]
    all_gather x1 -> x0, waiting for transfers between devices: 90.5 us -> none  [body(): shard_rows = lax.all_gather(rounded_rows, 'dp', axis=1, tiled=True)]
    reshape x0 -> x1, local copies, waits for them, and re-layouts: none -> 8.47 us  [body(): jnp.concatenate(lax.all_to_all(jnp.stack([rounded_rows] * lax.axis_size('...]
    all_to_all x0 -> x1, starting transfers between devices: none -> 6.63 us  [body(): lax.all_to_all(jnp.stack([rounded_rows] * lax.axis_size('dp')), 'dp', 0, 0)]
    all_to_all x1, starting transfers between devices: 32.8 us -> 39.3 us  [body(): lax.all_to_all(update_rows.reshape(slot_count, row_count, owner_count, co...]
  transfers between devices with their start and end apart: 3 -> 3, of which waited for: 2 -> 2; matrix products, arithmetic and copies ran while one was open for 3% -> 2% of each run, Pallas kernels for 0% -> 0%
where the time goes in v1:
time: 638 us
  waiting for transfers between devices  408 us (64%)
  blocking collectives  131 us (21%)
  starting transfers between devices  46 us (7%)
  matrix products  20.2 us (3%)
  local copies, waits for them, and re-layouts  14.5 us (2%)
  between operations  14.2 us (2%)
    reduce_scatter x1, waiting for transfers between devices, body(): lax.psum_scatter(grad_parts[0].astype(jnp.float32).astype(jnp.bfloat16),...  224 us
    all_to_all x1, waiting for transfers between devices, body(): lax.all_to_all(jnp.stack([rounded_rows] * lax.axis_size('dp')), 'dp', 0, 0)  183 us
    psum x1, blocking collectives, body(): lax.psum((square_adam, square_pre, vec_local), 'dp')  115 us
    all_to_all x1, starting transfers between devices, body(): lax.all_to_all(update_rows.reshape(slot_count, row_count, owner_count, co...  39.3 us
    all_to_all x1, blocking collectives, body(): lax.all_to_all(outgoing.astype(jnp.bfloat16), 'mp', split_axis=2, concat_...  16.5 us
  transfers between devices with their start and end apart: 3, of which 2 were waited for; matrix products, arithmetic and copies ran while one was open for 2% of the time, Pallas kernels for 0%

profile of v1, /device:TPU:1, one launch (start us, length us, event | category | flops | bytes accessed | tf_op | source)
XLA Modules:
  0.0 637.6 jit_solution(17236100801124281360)
XLA Ops:
  7.2 0.0 copy-start
  7.2 0.0 reduce-scatter.2.cloned.1.call-start
  7.2 0.7 reduce-scatter.2.cloned.1.call-update
  7.9 0.9 convert_reduce_fusion
  8.8 224.1 %reduce-scatter.2.cloned.1.call-done = bf16[16,32,128]{2,1,0:T(8,128)(2,1)} async-done(((bf16[16,1024,128]{2,1,0:T(8,128)(2,1)}), bf16[16,32,128]{2,1,0:T(8,128)(2,1)}) %reduce-scatter.2.cloned.1.call-update) | async-done | bytes 131088 | tf_op jit(solution)/shard_map/reduce_scatter | solution.py:44
  233.0 1.1 fusion.4
  234.2 16.5 %all_to_all.15 = bf16[4,32,8,128]{3,1,0,2:T(8,128)(2,1)S(1)} all-to-all(bf16[4,32,8,128]{3,1,0,2:T(8,128)(2,1)S(1)} %copy.32), channel_id=1, replica_groups=mesh['dp'=32,'mp'=8] {'mp'}, dimensions={2} | all-to-all | bytes 524288 | tf_op jit(solution)/shard_map/all_to_all | solution.py:52
  250.7 4.3 stack.2
  255.0 6.6 %all-to-all-start.1 = ((bf16[32,4,32,1024]{3,2,1,0:T(8,128)(2,1)}), bf16[32,4,32,1024]{3,2,1,0:T(8,128)(2,1)}, u32[]{:S(2)}, u32[]{:S(2)}) async-start(bf16[32,4,32,1024]{3,2,1,0:T(8,128)(2,1)} %stack.2), calls=%async_computation.2 | async-start | bytes 16777216 | tf_op jit(solution)/shard_map/all_to_all | solution.py:60
  261.7 0.1 dynamic-slice_reduce_fusion
  261.9 1.4 multiply_reduce_fusion.1
  263.2 183.4 %all-to-all-done.1 = bf16[32,4,32,1024]{3,2,1,0:T(8,128)(2,1)} async-done(((bf16[32,4,32,1024]{3,2,1,0:T(8,128)(2,1)}), bf16[32,4,32,1024]{3,2,1,0:T(8,128)(2,1)}, u32[]{:S(2)}, u32[]{:S(2)}) %all-to-all-start.1) | async-done | bytes 8388640 | tf_op jit(solution)/shard_map/all_to_all | solution.py:60
  446.6 8.5 %copy.34 = bf16[4,32,32,1024]{3,2,1,0:T(8,128)(2,1)} copy(bf16[4,32,32,1024]{3,2,0,1:T(8,128)(2,1)} %bitcast.6) | data formatting | bytes 16777216 | tf_op jit(solution)/shard_map/reshape | solution.py:59
  455.1 8.9 %multiply_reduce_fusion = (f32[4]{0:T(128)S(1)}, f32[4,32,1024]{2,1,0:T(8,128)S(1)}) fusion(bf16[4,1024,1024]{2,1,0:T(8,128)(2,1)} %param.16, bf16[4,32,1024]{2,1,0:T(8,128)(2,1)S(1)} %copy-done, bf16[4,1024,1024]{2,1,0:T(8,128)(2,1)} %bitcast.48), kind=kOutput, calls=%fused_computation.20 | convolution fusion | flops 537264128 | bytes 17563664 | tf_op jit(solution)/shard_map/crk,ckm->crm/dot_general | solution.py:82
  464.0 114.8 %all-reduce = (f32[4]{0:T(128)S(1)}, f32[4]{0:T(128)S(1)}, f32[9216]{0:T(1024)S(1)}) all-reduce(f32[4]{0:T(128)S(1)} %get-tuple-element.41, f32[4]{0:T(128)S(1)} %get-tuple-element.38, f32[9216]{0:T(1024)S(1)} %bitcast.54), channel_id=1, replica_groups=mesh['dp'=32,'mp'=8] {'dp'}, use_global_device_ids=true, to_apply=%region_6.7 | all-reduce | flops 9224 | bytes 73792 | tf_op jit(solution)/shard_map/psum | solution.py:91
  578.8 0.1 multiply_convert_fusion
  579.0 0.9 copy.35
  579.9 39.3 %all-to-all-start.2 = ((bf16[4,32,8,128]{3,0,1,2:T(4,128)(2,1)}), bf16[4,32,8,128]{3,0,1,2:T(4,128)(2,1)S(1)}, u32[]{:S(2)}, u32[]{:S(2)}) async-start(bf16[4,32,8,128]{3,0,1,2:T(4,128)(2,1)} %copy.35), calls=%async_computation.3 | async-start | bytes 524288 | tf_op jit(solution)/shard_map/all_to_all | solution.py:95
  619.2 0.0 copy-start.7
  619.2 6.5 %fusion.3 = f32[4,32,1024]{2,1,0:T(8,128)} fusion(f32[4,32,1024]{2,1,0:T(8,128)S(1)} %copy-done.5, bf16[4,1024,1024]{2,1,0:T(8,128)(2,1)} %bitcast.49, s32[]{:T(128)S(6)} %select_n.24, pred[4]{0:T(512)(128)(4,1)S(1)} %broadcast_compare_fusion), kind=kOutput, calls=%fused_computation.5 | convolution fusion | flops 268828672 | bytes 10485768 | tf_op jit(solution)/shard_map/cnr,cnk->crk/dot_general | solution.py:66
  625.7 3.4 fusion.1
  629.1 0.6 divide_convert_fusion
  629.8 0.3 fusion.5
  630.0 0.7 copy.38
  (26 shorter events, 0.2 us)
Async XLA Ops:
  7.2 447.9 %copy-start = (bf16[4,32,1024]{2,1,0:T(8,128)(2,1)S(1)}, bf16[4,32,1024]{2,1,0:T(8,128)(2,1)}, u32[]{:S(2)}) copy-start(bf16[4,32,1024]{2,1,0:T(8,128)(2,1)} %param.15) | copy-start | bytes 786436
  7.2 225.8 %reduce-scatter.2.cloned.1.call-start = ((), (), s32[]{:S(2)}) async-start(), calls=%async_computation.4 | async-start | bytes 4325376 | tf_op jit(solution)/shard_map/reduce_scatter | solution.py:44
  255.0 6.7 %copy-start.8 = (bf16[1,9216]{1,0:T(2,128)(2,1)S(1)}, bf16[1,9216]{1,0:T(2,128)(2,1)}, u32[]{:S(2)}) copy-start(bf16[1,9216]{1,0:T(2,128)(2,1)} %param.19) | copy-start | bytes 55300
  255.0 6.7 %copy-start.9 = (s32[16]{0:T(128)S(1)}, s32[16]{0:T(128)}, u32[]{:S(2)}) copy-start(s32[16]{0:T(128)} %param.12) | copy-start | bytes 196
  255.0 6.9 %copy-start.3 = (f32[4,32,1024]{2,1,0:T(8,128)S(1)}, f32[4,32,1024]{2,1,0:T(8,128)}, u32[]{:S(2)}) copy-start(f32[4,32,1024]{2,1,0:T(8,128)} %param.18) | copy-start | bytes 1572868
  255.0 6.9 %copy-start.4 = (f32[4,32,1024]{2,1,0:T(8,128)S(1)}, f32[4,32,1024]{2,1,0:T(8,128)}, u32[]{:S(2)}) copy-start(f32[4,32,1024]{2,1,0:T(8,128)} %param.17) | copy-start | bytes 1572868
  255.0 191.6 %all-to-all-start.1 = ((bf16[32,4,32,1024]{3,2,1,0:T(8,128)(2,1)}), bf16[32,4,32,1024]{3,2,1,0:T(8,128)(2,1)}, u32[]{:S(2)}, u32[]{:S(2)}) async-start(bf16[32,4,32,1024]{3,2,1,0:T(8,128)(2,1)} %stack.2), calls=%async_computation.2 | async-start | bytes 16777216 | tf_op jit(solution)/shard_map/all_to_all | solution.py:60
  455.1 164.1 %copy-start.5 = (f32[4,32,1024]{2,1,0:T(8,128)S(1)}, f32[4,32,1024]{2,1,0:T(8,128)}, u32[]{:S(2)}) copy-start(f32[4,32,1024]{2,1,0:T(8,128)} %param.14) | copy-start | bytes 1572868
  464.0 161.7 %copy-start.2 = (f32[4,32,1024]{2,1,0:T(8,128)S(1)}, f32[4,32,1024]{2,1,0:T(8,128)}, u32[]{:S(2)}) copy-start(f32[4,32,1024]{2,1,0:T(8,128)} %param.13) | copy-start | bytes 1572868
  579.9 49.9 %all-to-all-start.2 = ((bf16[4,32,8,128]{3,0,1,2:T(4,128)(2,1)}), bf16[4,32,8,128]{3,0,1,2:T(4,128)(2,1)S(1)}, u32[]{:S(2)}, u32[]{:S(2)}) async-start(bf16[4,32,8,128]{3,0,1,2:T(4,128)(2,1)} %copy.35), calls=%async_computation.3 | async-start | bytes 524288 | tf_op jit(solution)/shard_map/all_to_all | solution.py:95
  619.2 6.5 %copy-start.1 = (bf16[4,32,32,1024]{3,2,1,0:T(8,128)(2,1)S(1)}, bf16[4,32,32,1024]{3,2,1,0:T(8,128)(2,1)}, u32[]{:S(2)}) copy-start(bf16[4,32,32,1024]{3,2,1,0:T(8,128)(2,1)} %copy.34) | copy-start | bytes 25165828
  619.2 9.9 %copy-start.6 = (f32[9216]{0:T(1024)S(1)}, f32[9216]{0:T(1024)}, u32[]{:S(2)}) copy-start(f32[9216]{0:T(1024)} %param.21) | copy-start | bytes 110596
  619.2 9.9 %copy-start.7 = (f32[9216]{0:T(1024)S(1)}, f32[9216]{0:T(1024)}, u32[]{:S(2)}) copy-start(f32[9216]{0:T(1024)} %param.20) | copy-start | bytes 110596
Sparse Core Ops, SparseCore 0:
  11.9 221.0 reduce-scatter.1
